TPU v7x, 128 devices: a whole 4x4x4 slice. The times are simulated.
128 devices in a mesh: cell: 16 (over x, z_hi, core), tm: 8 (over y, z_lo).
Axes of the slice: x: 4, y: 4, z: 4 (z_hi: 2, z_lo: 2; z = z_hi * 2 + z_lo), core: 2. Of those that a mesh axis runs over, the one named last changes fastest.
Arguments:
- window: float32 [16384, 16384], P('cell', 'tm'), may hold values from -0.09375 to 0.09375
- range_test: float32 [16384, 256], P('tm'), may hold values from -0.046875 to 0.046875
- co_test: float32 [256, 16384], P(None, 'cell'), may hold values from -0.046875 to 0.046875
- core_left: float32 [512, 16384], P(None, 'cell'), may hold values from -0.046875 to 0.046875
- core_right: float32 [512, 16384], P(None, 'tm'), may hold values from -0.046875 to 0.046875
Outputs:
- range_basis: float32 [16384, 256], P('cell')
- co_basis: float32 [256, 16384], P(None, 'tm')
- core: float32 [256, 256], replicated
All inputs are finite; a program needn't handle non-finite values.
Results may differ from a plain program's by a relative error of at most 0.00023.
Values sent between devices are 32-bit elements; how exact they have to be, the bound alone decides.
A program may use at most 128 MiB of HBM per device.

v0:
```python
import math
import jax
import jax.numpy as jnp
from jax import lax
from jax.sharding import PartitionSpec as P


def inner_rows(left, right):
    return lax.dot_general(left, right, (((0,), (0,)), ((), ())), precision=lax.Precision.HIGHEST)


def inner_cols(left, right):
    return lax.dot_general(left, right, (((1,), (1,)), ((), ())), precision=lax.Precision.HIGHEST)


def product(left, right):
    return jnp.dot(left, right, precision=lax.Precision.HIGHEST, preferred_element_type=jnp.float32)


def per_device(window, range_test, co_test, core_left, core_right):
    rows_total = window.shape[0] * lax.axis_size("cell")
    cols_total = window.shape[1] * lax.axis_size("tm")
    range_term = product(window, range_test)
    co_term = product(co_test, window)
    left_window = product(core_left, window)
    core_term = inner_cols(left_window, core_right)
    sketch_z = lax.psum(core_term, ("cell", "tm"))
    range_full = lax.psum(range_term, "tm")
    co_full = lax.psum(co_term, "cell")
    gram_y = lax.psum(inner_rows(range_full, range_full) / rows_total, "cell")
    gram_w = lax.psum(inner_cols(co_full, co_full) / cols_total, "tm")
    lower_y = jnp.linalg.cholesky(gram_y)
    lower_w = jnp.linalg.cholesky(gram_w)
    range_basis = jax.scipy.linalg.solve_triangular(lower_y, range_full.T, lower=True).T
    co_basis = jax.scipy.linalg.solve_triangular(lower_w, co_full, lower=True)
    left_image = lax.psum(product(core_left, range_basis), "cell")
    right_image = lax.psum(inner_cols(core_right, co_basis), "tm")
    gram_left = inner_rows(left_image, left_image)
    gram_right = inner_rows(right_image, right_image)
    projected = inner_rows(left_image, sketch_z)
    left_solved = jax.scipy.linalg.cho_solve((jnp.linalg.cholesky(gram_left), True), projected)
    middle = product(left_solved, right_image)
    core = jax.scipy.linalg.cho_solve((jnp.linalg.cholesky(gram_right), True), middle.T).T
    core = core * math.sqrt(rows_total * cols_total)
    return (range_basis, co_basis, core)


def solution(mesh):
    return jax.shard_map(
        per_device,
        mesh=mesh,
        in_specs=(P("cell", "tm"), P("tm", None), P(None, "cell"), P(None, "cell"), P(None, "tm")),
        out_specs=(P("cell", None), P(None, "tm"), P()),
        check_vma=False,
    )
```

profile of v0, /device:TPU:0, one launch (start us, length us, event | category | flops | bytes accessed | tf_op | source)
XLA Modules:
  0.0 920.8 jit_solution(13198876106782574047)
XLA Ops:
  7.2 10.7 %fusion.50 = f32[1024,256]{1,0:T(8,128)} fusion(f32[1024,2048]{1,0:T(8,128)} %param.6, f32[2048,256]{1,0:T(8,128)} %param.7), kind=kOutput, calls=%fused_computation.123 | convolution fusion | flops 6442450944 | bytes 11534336 | tf_op jit(solution)/shard_map/dot_general | solution.py:17
  18.0 80.7 %all-reduce.9.cloned.1.call-done = f32[1024,256]{1,0:T(8,128)} async-done(((f32[1024,256]{1,0:T(8,128)}), f32[1024,256]{1,0:T(8,128)}) %all-reduce.9.cloned.1.call-update) | async-done | bytes 1048592 | tf_op jit(solution)/shard_map/psum | solution.py:28
  98.6 4.1 convolution_multiply_fusion.1
  102.8 10.7 %fusion.51 = f32[256,2048]{1,0:T(8,128)} fusion(f32[256,1024]{1,0:T(8,128)S(1)} %copy-done.12, f32[1024,2048]{1,0:T(8,128)} %param.6), kind=kOutput, calls=%fused_computation.124 | convolution fusion | flops 6442450944 | bytes 11534336 | tf_op jit(solution)/shard_map/dot_general | solution.py:17
  113.5 127.4 %all-reduce.11.cloned.1.call-done = f32[256,256]{0,1:T(8,128)} async-done(((f32[256,256]{0,1:T(8,128)}), f32[256,256]{0,1:T(8,128)}) %all-reduce.11.cloned.1.call-update) | async-done | bytes 262160 | tf_op jit(solution)/shard_map/psum | solution.py:30
  240.9 1.1 copy.9
  242.0 1.0 fusion.15
  243.7 11.7 %cholesky.214 = f32[128,128]{1,0:T(8,128)S(1)} custom-call(f32[128,128]{1,0:T(8,128)S(1)} %cholesky.346), custom_call_target="Cholesky" | custom-call | tf_op jit(solution)/shard_map/jit(cholesky)/cholesky | solution.py:32
  255.5 9.8 %custom-call.37 = f32[1,128,128]{1,2,0:T(8,128)S(1)} custom-call(f32[1,128,128]{2,1,0:T(8,128)S(1)} %get-tuple-element.96), custom_call_target="InvertDiagBlocksLowerTriangular" | custom-call | tf_op jit(solution)/shard_map/jit(cholesky)/cholesky | solution.py:32
  265.3 1.0 constant_dynamic-update-slice_fusion.7
  266.3 1.1 convolution_subtract_fusion.9
  267.4 11.7 %cholesky.231 = f32[128,128]{1,0:T(8,128)S(1)} custom-call(f32[128,128]{1,0:T(8,128)S(1)} %convolution_subtract_fusion.9), custom_call_target="Cholesky" | custom-call | tf_op jit(solution)/shard_map/jit(cholesky)/cholesky | solution.py:32
  282.3 4.1 while.4
  282.9 1.4 bitcast_dynamic-update-slice_fusion.8
  284.9 1.4 bitcast_dynamic-update-slice_fusion.8
  287.0 20.7 %custom-call.30 = f32[2,128,128]{1,2,0:T(8,128)S(1)} custom-call(f32[2,128,128]{2,1,0:T(8,128)} %copy-done.17), custom_call_target="InvertDiagBlocksLowerTriangular" | custom-call | tf_op jit(solution)/shard_map/jit(_solve_triangular)/triangular_solve | solution.py:34
  308.4 1.0 convolution_subtract_fusion.1
  310.0 2.8 convolution_bitcast_fusion
  312.9 16.9 %fusion.54 = f32[512,2048]{1,0:T(8,128)S(1)} fusion(f32[512,1024]{1,0:T(8,128)S(1)} %copy-done, f32[1024,2048]{1,0:T(8,128)} %param.6), kind=kOutput, calls=%fused_computation.127 | convolution fusion | flops 12884901888 | bytes 14680064 | tf_op jit(solution)/shard_map/dot_general | solution.py:17
  329.8 7.9 fusion.55
  337.7 2.8 all-reduce.13.cloned.1.call-start
  340.5 1.0 fusion.2
  341.6 2.5 copy.14
  344.1 116.8 %all-reduce.19.cloned.1.call-done = (f32[256,2048]{1,0:T(8,128)}, f32[512,256]{0,1:T(8,128)}) async-done(((f32[256,2048]{1,0:T(8,128)}, f32[512,256]{0,1:T(8,128)}), (f32[256,2048]{1,0:T(8,128)}, f32[512,256]{0,1:T(8,128)})) %all-reduce.19.cloned.1.call-update) | async-done | bytes 2621456 | tf_op jit(solution)/shard_map/psum | solution.py:29
  460.9 1.8 fusion.53
  462.9 11.7 %cholesky.316 = f32[128,128]{1,0:T(8,128)S(1)} custom-call(f32[128,128]{1,0:T(8,128)S(1)} %cholesky.355), custom_call_target="Cholesky" | custom-call | tf_op jit(solution)/shard_map/jit(cholesky)/cholesky | solution.py:41
  474.7 9.8 %custom-call.40 = f32[1,128,128]{1,2,0:T(8,128)S(1)} custom-call(f32[1,128,128]{2,1,0:T(8,128)S(1)} %get-tuple-element.88), custom_call_target="InvertDiagBlocksLowerTriangular" | custom-call | tf_op jit(solution)/shard_map/jit(cholesky)/cholesky | solution.py:41
  485.0 11.7 %cholesky.333 = f32[128,128]{1,0:T(8,128)S(1)} custom-call(f32[128,128]{1,0:T(8,128)S(1)} %convolution_subtract_fusion.6), custom_call_target="Cholesky" | custom-call | tf_op jit(solution)/shard_map/jit(cholesky)/cholesky | solution.py:41
  499.5 4.1 while.7
  500.1 1.4 bitcast_dynamic-update-slice_fusion.11
  502.2 1.4 bitcast_dynamic-update-slice_fusion.11
  503.6 19.7 %custom-call.33 = f32[2,128,128]{1,2,0:T(8,128)S(1)} custom-call(f32[2,128,128]{2,1,0:T(8,128)S(1)} %get-tuple-element.35), custom_call_target="InvertDiagBlocksLowerTriangular" | custom-call | tf_op jit(solution)/shard_map/jit(_cho_solve)/triangular_solve | solution.py:41
  523.3 4.8 convolution_multiply_fusion
  528.6 85.9 %all-reduce.17.cloned.1.call-done = f32[512,512]{1,0:T(8,128)} async-done(((f32[512,512]{1,0:T(8,128)}), f32[512,512]{1,0:T(8,128)}) %all-reduce.17.cloned.1.call-update) | async-done | bytes 1048592 | tf_op jit(solution)/shard_map/psum | solution.py:27
  614.5 2.3 fusion.56
  618.1 73.0 %all-reduce.13.cloned.1.call-done = f32[256,256]{0,1:T(8,128)} async-done(((f32[256,256]{0,1:T(8,128)}), f32[256,256]{0,1:T(8,128)}) %all-reduce.13.cloned.1.call-update) | async-done | bytes 262160 | tf_op jit(solution)/shard_map/psum | solution.py:31
  691.1 1.1 copy.11
  692.2 1.0 fusion.14
  693.2 11.7 %cholesky.248 = f32[128,128]{1,0:T(8,128)S(1)} custom-call(f32[128,128]{1,0:T(8,128)S(1)} %cholesky.349), custom_call_target="Cholesky" | custom-call | tf_op jit(solution)/shard_map/jit(cholesky)/cholesky | solution.py:33
  705.0 9.8 %custom-call.38 = f32[1,128,128]{1,2,0:T(8,128)S(1)} custom-call(f32[1,128,128]{2,1,0:T(8,128)S(1)} %get-tuple-element.92), custom_call_target="InvertDiagBlocksLowerTriangular" | custom-call | tf_op jit(solution)/shard_map/jit(cholesky)/cholesky | solution.py:33
  714.8 1.0 constant_dynamic-update-slice_fusion.5
  715.8 1.1 convolution_subtract_fusion.8
  716.9 11.9 %cholesky.265 = f32[128,128]{1,0:T(8,128)S(1)} custom-call(f32[128,128]{1,0:T(8,128)S(1)} %convolution_subtract_fusion.8), custom_call_target="Cholesky" | custom-call | tf_op jit(solution)/shard_map/jit(cholesky)/cholesky | solution.py:33
  731.5 4.0 while.5
  732.1 1.4 bitcast_dynamic-update-slice_fusion.9
  734.1 1.4 bitcast_dynamic-update-slice_fusion.9
  735.5 19.7 %custom-call.31 = f32[2,128,128]{1,2,0:T(8,128)S(1)} custom-call(f32[2,128,128]{2,1,0:T(8,128)S(1)} %get-tuple-element.19), custom_call_target="InvertDiagBlocksLowerTriangular" | custom-call | tf_op jit(solution)/shard_map/jit(_solve_triangular)/triangular_solve | solution.py:35
  755.2 2.4 fusion
  757.6 1.0 convolution_subtract_fusion
  758.6 1.1 fusion.23
  759.9 1.3 copy-done.7
  761.2 1.4 copy-done.3
  762.6 4.5 convolution_bitcast_fusion.1
  768.3 73.2 %all-reduce.15.cloned.1.call-done = f32[512,256]{0,1:T(8,128)} async-done(((f32[512,256]{0,1:T(8,128)}), f32[512,256]{0,1:T(8,128)}) %all-reduce.15.cloned.1.call-update) | async-done | bytes 524304 | tf_op jit(solution)/shard_map/psum | solution.py:37
  841.5 1.8 fusion.52
  845.9 11.9 %cholesky.282 = f32[128,128]{1,0:T(8,128)S(1)} custom-call(f32[128,128]{1,0:T(8,128)S(1)} %cholesky.352), custom_call_target="Cholesky" | custom-call | tf_op jit(solution)/shard_map/jit(cholesky)/cholesky | solution.py:43
  857.8 9.8 %custom-call.39 = f32[1,128,128]{1,2,0:T(8,128)S(1)} custom-call(f32[1,128,128]{2,1,0:T(8,128)S(1)} %get-tuple-element.84), custom_call_target="InvertDiagBlocksLowerTriangular" | custom-call | tf_op jit(solution)/shard_map/jit(cholesky)/cholesky | solution.py:43
  867.7 1.0 constant_dynamic-update-slice_fusion.3
  868.7 1.1 convolution_subtract_fusion.7
  869.8 11.7 %cholesky.299 = f32[128,128]{1,0:T(8,128)S(1)} custom-call(f32[128,128]{1,0:T(8,128)S(1)} %convolution_subtract_fusion.7), custom_call_target="Cholesky" | custom-call | tf_op jit(solution)/shard_map/jit(cholesky)/cholesky | solution.py:43
  885.2 4.1 while.6
  885.8 1.4 bitcast_dynamic-update-slice_fusion.10
  887.9 1.4 bitcast_dynamic-update-slice_fusion.10
  890.0 20.5 %custom-call.32 = f32[2,128,128]{1,2,0:T(8,128)S(1)} custom-call(f32[2,128,128]{2,1,0:T(8,128)} %copy-done.16), custom_call_target="InvertDiagBlocksLowerTriangular" | custom-call | tf_op jit(solution)/shard_map/jit(_cho_solve)/triangular_solve | solution.py:43
  (118 shorter events, 25.0 us)
Async XLA Ops:
  7.2 302.9 %copy-start = (f32[512,1024]{1,0:T(8,128)S(1)}, f32[512,1024]{1,0:T(8,128)}, u32[]{:S(2)}) copy-start(f32[512,1024]{1,0:T(8,128)} %param.9) | copy-start | bytes 6291460
  7.2 91.5 %all-reduce.9.cloned.1.call-start = ((), (), s32[]{:S(2)}) async-start(), calls=%async_computation | async-start | bytes 2097152 | tf_op jit(solution)/shard_map/psum | solution.py:28
  17.9 84.9 %copy-start.12 = (f32[256,1024]{1,0:T(8,128)S(1)}, f32[256,1024]{1,0:T(8,128)}, u32[]{:S(2)}) copy-start(f32[256,1024]{1,0:T(8,128)} %param.8) | copy-start | bytes 3145732
  17.9 223.0 %all-reduce.11.cloned.1.call-start = ((), (), s32[]{:S(2)}) async-start(), calls=%async_computation.1 | async-start | bytes 524288 | tf_op jit(solution)/shard_map/psum | solution.py:30
  102.7 358.2 %all-reduce.19.cloned.1.call-start = ((), (), s32[]{:S(2)}) async-start(), calls=%async_computation.5 | async-start | bytes 5242880 | tf_op jit(solution)/shard_map/psum | solution.py:29
  113.5 194.2 %copy-start.4 = (f32[1024,256]{1,0:T(8,128)S(1)}, f32[1024,256]{1,0:T(8,128)}, u32[]{:S(2)}) copy-start(f32[1024,256]{1,0:T(8,128)} %all-reduce.9.cloned.1.call-done) | copy-start | bytes 3145732
  243.0 0.7 copy-start.13
  279.2 2.0 copy-start.10
  286.4 0.7 copy-start.17
  308.4 1.7 copy-start.5
  312.8 301.7 %all-reduce.17.cloned.1.call-start = ((), (), s32[]{:S(2)}) async-start(), calls=%async_computation.4 | async-start | bytes 2097152 | tf_op jit(solution)/shard_map/psum | solution.py:27
  312.9 16.9 %copy-start.2 = (f32[512,2048]{1,0:T(8,128)S(1)}, f32[512,2048]{1,0:T(8,128)}, u32[]{:S(2)}) copy-start(f32[512,2048]{1,0:T(8,128)} %param.10) | copy-start | bytes 12582916
  329.8 10.7 %copy-start.6 = (f32[128,1024]{1,0:T(8,128)S(1)}, f32[128,1024]{1,0:T(8,128)}, u32[]{:S(2)}) copy-start(f32[128,1024]{1,0:T(8,128)} %copy-done.5) | copy-start | bytes 1572868
  337.7 353.3 %all-reduce.13.cloned.1.call-start = ((), (), s32[]{:S(2)}) async-start(), calls=%async_computation.2 | async-start | bytes 524288 | tf_op jit(solution)/shard_map/psum | solution.py:31
  523.3 91.3 %copy-start.9 = (f32[512,256]{0,1:T(8,128)S(1)}, f32[512,256]{0,1:T(8,128)}, u32[]{:S(2)}) copy-start(f32[512,256]{0,1:T(8,128)} %get-tuple-element.72) | copy-start | bytes 1572868
  528.2 313.4 %all-reduce.15.cloned.1.call-start = ((), (), s32[]{:S(2)}) async-start(), calls=%async_computation.3 | async-start | bytes 1048576 | tf_op jit(solution)/shard_map/psum | solution.py:37
  693.2 11.7 %copy-start.14 = (f32[256,256]{1,0:T(8,128)}, f32[256,256]{1,0:T(8,128)S(1)}, u32[]{:S(2)}) copy-start(f32[256,256]{1,0:T(8,128)S(1)} %fusion.14) | copy-start | bytes 786436
  755.2 2.4 copy-start.1
  759.7 2.9 copy-start.3
  759.9 1.3 copy-start.7
  843.3 67.1 %copy-start.8 = (f32[512,256]{0,1:T(8,128)S(1)}, f32[512,256]{0,1:T(8,128)}, u32[]{:S(2)}) copy-start(f32[512,256]{0,1:T(8,128)} %all-reduce.15.cloned.1.call-done) | copy-start | bytes 1572868
  845.2 0.7 copy-start.15
  882.3 1.9 copy-start.11
  889.3 0.7 copy-start.16
Sparse Core Ops, SparseCore 0:
  18.1 80.5 all-reduce.8
  102.8 138.0 all-reduce.10
  313.0 147.9 all-reduce.18
  465.6 148.9 all-reduce.16
  617.4 73.6 all-reduce.12
  767.3 74.1 all-reduce.14
where the time goes:
time: 929 us; the launch traced here: 921 us
  waiting for transfers between devices  557 us (60%)
  other arithmetic  225 us (24%)
  matrix products  86.6 us (9%)
  local copies, waits for them, and re-layouts  28.3 us (3%)
  between operations  20.2 us (2%)
    psum x1, waiting for transfers between devices, per_device(): gram_y = lax.psum(inner_rows(range_full, range_full) / rows_total, 'cell')  127 us
    psum x1, waiting for transfers between devices, per_device(): co_full = lax.psum(co_term, 'cell')  117 us
    psum x1, waiting for transfers between devices, per_device(): sketch_z = lax.psum(core_term, ('cell', 'tm'))  85.9 us
    psum x1, waiting for transfers between devices, per_device(): range_full = lax.psum(range_term, 'tm')  80.7 us
    psum x1, waiting for transfers between devices, per_device(): right_image = lax.psum(inner_cols(core_right, co_basis), 'tm')  73.2 us
    psum x1, waiting for transfers between devices, per_device(): gram_w = lax.psum(inner_cols(co_full, co_full) / cols_total, 'tm')  73 us
    dot_general x5, matrix products, product(): jnp.dot(left, right, precision=lax.Precision.HIGHEST, preferred_element_t...  41.6 us
    another operation x7, other arithmetic, per_device(): jnp.linalg.cholesky(gram_right)  34.8 us
  transfers between devices with their start and end apart: 6, of which 6 were waited for; matrix products, arithmetic and copies ran while one was open for 12% of the time, Pallas kernels for 0%

commit v1 on v0

--- a/solution.py
+++ b/solution.py
@@ -24,7 +24,7 @@
     co_term = product(co_test, window)
     left_window = product(core_left, window)
     core_term = inner_cols(left_window, core_right)
-    sketch_z = lax.psum(core_term, ("cell", "tm"))
+    sketch_z = lax.psum(lax.psum(core_term, "cell"), "tm")
     range_full = lax.psum(range_term, "tm")
     co_full = lax.psum(co_term, "cell")
     gram_y = lax.psum(inner_rows(range_full, range_full) / rows_total, "cell")

time: 929 us -> 791 us (0.85)
  waiting for transfers between devices: 557 us -> 428 us
    psum x1 -> x0, waiting for transfers between devices: 85.9 us -> none  [per_device(): sketch_z = lax.psum(core_term, ('cell', 'tm'))]
    psum x1, waiting for transfers between devices: 117 us -> 148 us  [per_device(): co_full = lax.psum(co_term, 'cell')]
    psum x1, waiting for transfers between devices: 80.7 us -> 54.6 us  [per_device(): range_full = lax.psum(range_term, 'tm')]
    psum x1, waiting for transfers between devices: 73.2 us -> 48.1 us  [per_device(): right_image = lax.psum(inner_cols(core_right, co_basis), 'tm')]
    psum x1, waiting for transfers between devices: 73 us -> 50.2 us  [per_device(): gram_w = lax.psum(inner_cols(co_full, co_full) / cols_total, 'tm')]
  transfers between devices with their start and end apart: 6 -> 5, of which waited for: 6 -> 5; matrix products, arithmetic and copies ran while one was open for 12% -> 13% of each run, Pallas kernels for 0% -> 0%
where the time goes in v1:
time: 791 us; the launch traced here: 787 us
  waiting for transfers between devices  428 us (54%)
  other arithmetic  223 us (28%)
  matrix products  87.9 us (11%)
  local copies, waits for them, and re-layouts  27.1 us (3%)
  between operations  19.6 us (2%)
    psum x1, waiting for transfers between devices, per_device(): co_full = lax.psum(co_term, 'cell')  148 us
    psum x1, waiting for transfers between devices, per_device(): gram_y = lax.psum(inner_rows(range_full, range_full) / rows_total, 'cell')  128 us
    psum x1, waiting for transfers between devices, per_device(): range_full = lax.psum(range_term, 'tm')  54.6 us
    psum x1, waiting for transfers between devices, per_device(): gram_w = lax.psum(inner_cols(co_full, co_full) / cols_total, 'tm')  50.2 us
    psum x1, waiting for transfers between devices, per_device(): right_image = lax.psum(inner_cols(core_right, co_basis), 'tm')  48.1 us
    dot_general x5, matrix products, product(): jnp.dot(left, right, precision=lax.Precision.HIGHEST, preferred_element_t...  40.1 us
    another operation x7, other arithmetic, per_device(): lower_w = jnp.linalg.cholesky(gram_w)  34.8 us
    another operation x7, other arithmetic, per_device(): jnp.linalg.cholesky(gram_right)  34.6 us
  transfers between devices with their start and end apart: 5, of which 5 were waited for; matrix products, arithmetic and copies ran while one was open for 13% of the time, Pallas kernels for 0%

profile of v1, /device:TPU:0, one launch (start us, length us, event | category | flops | bytes accessed | tf_op | source)
XLA Modules:
  0.0 786.8 jit_solution(13894511482792279274)
XLA Ops:
  7.2 10.7 %fusion.50 = f32[1024,256]{1,0:T(8,128)} fusion(f32[1024,2048]{1,0:T(8,128)} %param.6, f32[2048,256]{1,0:T(8,128)} %param.7), kind=kOutput, calls=%fused_computation.123 | convolution fusion | flops 6442450944 | bytes 11534336 | tf_op jit(solution)/shard_map/dot_general | solution.py:17
  18.2 10.7 %fusion.51 = f32[256,2048]{1,0:T(8,128)} fusion(f32[256,1024]{1,0:T(8,128)S(1)} %copy-done.11, f32[1024,2048]{1,0:T(8,128)} %param.6), kind=kOutput, calls=%fused_computation.124 | convolution fusion | flops 6442450944 | bytes 11534336 | tf_op jit(solution)/shard_map/dot_general | solution.py:17
  29.0 15.2 %fusion.54 = f32[512,2048]{1,0:T(8,128)} fusion(f32[512,1024]{1,0:T(8,128)S(1)} %copy-done, f32[1024,2048]{1,0:T(8,128)S(1)} %copy-done.1), kind=kOutput, calls=%fused_computation.127 | convolution fusion | flops 12884901888 | bytes 14680064 | tf_op jit(solution)/shard_map/dot_general | solution.py:17
  44.2 54.6 %all-reduce.9.cloned.1.call-done = f32[1024,256]{1,0:T(8,128)} async-done(((f32[1024,256]{1,0:T(8,128)}), f32[1024,256]{1,0:T(8,128)}) %all-reduce.9.cloned.1.call-update) | async-done | bytes 1048592 | tf_op jit(solution)/shard_map/psum | solution.py:28
  98.8 4.1 convolution_multiply_fusion.1
  103.1 10.3 %fusion.55 = f32[512,512]{1,0:T(8,128)} fusion(f32[512,2048]{1,0:T(8,128)} %fusion.54, f32[512,2048]{1,0:T(8,128)} %param.10), kind=kOutput, calls=%fused_computation.128 | convolution fusion | flops 6442450944 | bytes 9437184 | tf_op jit(solution)/shard_map/dot_general | solution.py:13
  113.4 127.6 %all-reduce.11.cloned.1.call-done = f32[256,256]{0,1:T(8,128)} async-done(((f32[256,256]{0,1:T(8,128)}), f32[256,256]{0,1:T(8,128)}) %all-reduce.11.cloned.1.call-update) | async-done | bytes 262160 | tf_op jit(solution)/shard_map/psum | solution.py:30
  241.1 1.1 copy.9
  242.1 1.0 fusion.15
  243.8 11.7 %cholesky.214 = f32[128,128]{1,0:T(8,128)S(1)} custom-call(f32[128,128]{1,0:T(8,128)S(1)} %cholesky.346), custom_call_target="Cholesky" | custom-call | tf_op jit(solution)/shard_map/jit(cholesky)/cholesky | solution.py:32
  255.6 9.8 %custom-call.37 = f32[1,128,128]{1,2,0:T(8,128)S(1)} custom-call(f32[1,128,128]{2,1,0:T(8,128)S(1)} %get-tuple-element.99), custom_call_target="InvertDiagBlocksLowerTriangular" | custom-call | tf_op jit(solution)/shard_map/jit(cholesky)/cholesky | solution.py:32
  265.4 1.0 constant_dynamic-update-slice_fusion.7
  266.5 1.1 convolution_subtract_fusion.9
  267.6 11.7 %cholesky.231 = f32[128,128]{1,0:T(8,128)S(1)} custom-call(f32[128,128]{1,0:T(8,128)S(1)} %convolution_subtract_fusion.9), custom_call_target="Cholesky" | custom-call | tf_op jit(solution)/shard_map/jit(cholesky)/cholesky | solution.py:32
  281.2 1.0 select_select_fusion.3
  282.3 3.9 while.4
  282.9 1.3 bitcast_dynamic-update-slice_fusion.8
  284.9 1.3 bitcast_dynamic-update-slice_fusion.8
  286.8 20.9 %custom-call.30 = f32[2,128,128]{1,2,0:T(8,128)S(1)} custom-call(f32[2,128,128]{2,1,0:T(8,128)} %copy-done.16), custom_call_target="InvertDiagBlocksLowerTriangular" | custom-call | tf_op jit(solution)/shard_map/jit(_solve_triangular)/triangular_solve | solution.py:34
  308.4 1.0 convolution_subtract_fusion.1
  310.1 2.8 convolution_bitcast_fusion
  312.9 1.0 copy-done.6
  313.9 1.1 fusion.2
  314.9 2.5 copy.14
  317.4 147.7 %all-reduce.15.cloned.1.call-done = (f32[256,2048]{1,0:T(8,128)}, f32[512,256]{0,1:T(8,128)}, f32[512,512]{1,0:T(8,128)}) async-done(((f32[256,2048]{1,0:T(8,128)}, f32[512,256]{0,1:T(8,128)}, f32[512,512]{1,0:T(8,128)}), (f32[256,2048]{1,0:T(8,128)}, f32[512,256]{0,1:T(8,128)}, f32[512,512]{1,0:T(8,128)})) %all-reduce.15.cloned.1.call-update) | async-done | bytes 3670032 | tf_op jit(solution)/shard_map/psum | solution.py:29
  465.2 4.8 convolution_multiply_fusion
  471.8 11.7 %cholesky.316 = f32[128,128]{1,0:T(8,128)S(1)} custom-call(f32[128,128]{1,0:T(8,128)S(1)} %cholesky.355), custom_call_target="Cholesky" | custom-call | tf_op jit(solution)/shard_map/jit(cholesky)/cholesky | solution.py:41
  483.6 9.8 %custom-call.40 = f32[1,128,128]{1,2,0:T(8,128)S(1)} custom-call(f32[1,128,128]{2,1,0:T(8,128)S(1)} %get-tuple-element.91), custom_call_target="InvertDiagBlocksLowerTriangular" | custom-call | tf_op jit(solution)/shard_map/jit(cholesky)/cholesky | solution.py:41
  493.4 1.0 constant_dynamic-update-slice_fusion.1
  494.4 50.2 %all-reduce.13.cloned.1.call-done = f32[256,256]{0,1:T(8,128)} async-done(((f32[256,256]{0,1:T(8,128)}), f32[256,256]{0,1:T(8,128)}) %all-reduce.13.cloned.1.call-update) | async-done | bytes 262160 | tf_op jit(solution)/shard_map/psum | solution.py:31
  544.6 1.1 copy.11
  545.7 1.0 fusion.14
  546.7 11.7 %cholesky.248 = f32[128,128]{1,0:T(8,128)S(1)} custom-call(f32[128,128]{1,0:T(8,128)S(1)} %cholesky.349), custom_call_target="Cholesky" | custom-call | tf_op jit(solution)/shard_map/jit(cholesky)/cholesky | solution.py:33
  558.5 10.0 %custom-call.38 = f32[1,128,128]{1,2,0:T(8,128)S(1)} custom-call(f32[1,128,128]{2,1,0:T(8,128)S(1)} %get-tuple-element.95), custom_call_target="InvertDiagBlocksLowerTriangular" | custom-call | tf_op jit(solution)/shard_map/jit(cholesky)/cholesky | solution.py:33
  568.4 1.0 constant_dynamic-update-slice_fusion.5
  569.5 1.1 convolution_subtract_fusion.8
  570.6 11.7 %cholesky.265 = f32[128,128]{1,0:T(8,128)S(1)} custom-call(f32[128,128]{1,0:T(8,128)S(1)} %convolution_subtract_fusion.8), custom_call_target="Cholesky" | custom-call | tf_op jit(solution)/shard_map/jit(cholesky)/cholesky | solution.py:33
  585.0 4.0 while.5
  585.6 1.4 bitcast_dynamic-update-slice_fusion.9
  587.6 1.4 bitcast_dynamic-update-slice_fusion.9
  589.0 20.1 %custom-call.31 = f32[2,128,128]{1,2,0:T(8,128)S(1)} custom-call(f32[2,128,128]{2,1,0:T(8,128)S(1)} %get-tuple-element.19), custom_call_target="InvertDiagBlocksLowerTriangular" | custom-call | tf_op jit(solution)/shard_map/jit(_solve_triangular)/triangular_solve | solution.py:35
  609.1 2.4 fusion
  611.5 1.0 convolution_subtract_fusion
  612.5 1.1 fusion.23
  613.8 2.0 copy-done.3
  615.8 4.5 convolution_bitcast_fusion.1
  620.3 1.1 convolution_subtract_fusion.6
  621.4 11.7 %cholesky.333 = f32[128,128]{1,0:T(8,128)S(1)} custom-call(f32[128,128]{1,0:T(8,128)S(1)} %convolution_subtract_fusion.6), custom_call_target="Cholesky" | custom-call | tf_op jit(solution)/shard_map/jit(cholesky)/cholesky | solution.py:41
  635.7 3.8 while.7
  636.3 1.3 bitcast_dynamic-update-slice_fusion.11
  638.2 1.3 bitcast_dynamic-update-slice_fusion.11
  639.5 19.8 %custom-call.33 = f32[2,128,128]{1,2,0:T(8,128)S(1)} custom-call(f32[2,128,128]{2,1,0:T(8,128)S(1)} %get-tuple-element.35), custom_call_target="InvertDiagBlocksLowerTriangular" | custom-call | tf_op jit(solution)/shard_map/jit(_cho_solve)/triangular_solve | solution.py:41
  659.3 48.1 %all-reduce.17.cloned.1.call-done = (f32[512,256]{0,1:T(8,128)}, f32[512,512]{1,0:T(8,128)}) async-done(((f32[512,256]{0,1:T(8,128)}, f32[512,512]{1,0:T(8,128)}), (f32[512,256]{0,1:T(8,128)}, f32[512,512]{1,0:T(8,128)})) %all-reduce.17.cloned.1.call-update) | async-done | bytes 1572880 | tf_op jit(solution)/shard_map/psum | solution.py:37
  707.4 1.8 fusion.52
  710.2 11.7 %cholesky.282 = f32[128,128]{1,0:T(8,128)S(1)} custom-call(f32[128,128]{1,0:T(8,128)S(1)} %cholesky.352), custom_call_target="Cholesky" | custom-call | tf_op jit(solution)/shard_map/jit(cholesky)/cholesky | solution.py:43
  721.9 9.8 %custom-call.39 = f32[1,128,128]{1,2,0:T(8,128)S(1)} custom-call(f32[1,128,128]{2,1,0:T(8,128)S(1)} %get-tuple-element.87), custom_call_target="InvertDiagBlocksLowerTriangular" | custom-call | tf_op jit(solution)/shard_map/jit(cholesky)/cholesky | solution.py:43
  731.7 1.0 constant_dynamic-update-slice_fusion.3
  732.8 1.1 convolution_subtract_fusion.7
  733.9 11.7 %cholesky.299 = f32[128,128]{1,0:T(8,128)S(1)} custom-call(f32[128,128]{1,0:T(8,128)S(1)} %convolution_subtract_fusion.7), custom_call_target="Cholesky" | custom-call | tf_op jit(solution)/shard_map/jit(cholesky)/cholesky | solution.py:43
  748.3 3.9 while.6
  748.9 1.3 bitcast_dynamic-update-slice_fusion.10
  750.8 1.3 bitcast_dynamic-update-slice_fusion.10
  752.2 19.9 %custom-call.32 = f32[2,128,128]{1,2,0:T(8,128)S(1)} custom-call(f32[2,128,128]{2,1,0:T(8,128)S(1)} %get-tuple-element.27), custom_call_target="InvertDiagBlocksLowerTriangular" | custom-call | tf_op jit(solution)/shard_map/jit(_cho_solve)/triangular_solve | solution.py:43
  772.1 2.3 fusion.56
  (113 shorter events, 21.4 us)
Async XLA Ops:
  7.2 21.8 %copy-start = (f32[512,1024]{1,0:T(8,128)S(1)}, f32[512,1024]{1,0:T(8,128)}, u32[]{:S(2)}) copy-start(f32[512,1024]{1,0:T(8,128)} %param.9) | copy-start | bytes 6291460
  7.2 11.0 %copy-start.11 = (f32[256,1024]{1,0:T(8,128)S(1)}, f32[256,1024]{1,0:T(8,128)}, u32[]{:S(2)}) copy-start(f32[256,1024]{1,0:T(8,128)} %param.8) | copy-start | bytes 3145732
  7.2 91.6 %all-reduce.9.cloned.1.call-start = ((), (), s32[]{:S(2)}) async-start(), calls=%async_computation | async-start | bytes 2097152 | tf_op jit(solution)/shard_map/psum | solution.py:28
  18.0 223.1 %all-reduce.11.cloned.1.call-start = ((), (), s32[]{:S(2)}) async-start(), calls=%async_computation.1 | async-start | bytes 524288 | tf_op jit(solution)/shard_map/psum | solution.py:30
  18.2 10.7 %copy-start.1 = (f32[1024,2048]{1,0:T(8,128)S(1)}, f32[1024,2048]{1,0:T(8,128)}, u32[]{:S(2)}) copy-start(f32[1024,2048]{1,0:T(8,128)} %param.6) | copy-start | bytes 25165828
  102.9 362.3 %all-reduce.15.cloned.1.call-start = ((), (), s32[]{:S(2)}) async-start(), calls=%async_computation.3 | async-start | bytes 7340032 | tf_op jit(solution)/shard_map/psum | solution.py:29
  113.4 194.3 %copy-start.4 = (f32[1024,256]{1,0:T(8,128)S(1)}, f32[1024,256]{1,0:T(8,128)}, u32[]{:S(2)}) copy-start(f32[1024,256]{1,0:T(8,128)} %all-reduce.9.cloned.1.call-done) | copy-start | bytes 3145732
  243.1 0.7 copy-start.13
  279.4 1.9 copy-start.10
  286.2 0.7 copy-start.16
  308.4 1.7 copy-start.5
  312.8 1.0 copy-start.6
  312.8 231.7 %all-reduce.13.cloned.1.call-start = ((), (), s32[]{:S(2)}) async-start(), calls=%async_computation.2 | async-start | bytes 524288 | tf_op jit(solution)/shard_map/psum | solution.py:31
  465.2 5.1 copy-start.9
  470.0 237.4 %all-reduce.17.cloned.1.call-start = ((), (), s32[]{:S(2)}) async-start(), calls=%async_computation.4 | async-start | bytes 3145728 | tf_op jit(solution)/shard_map/psum | solution.py:37
  471.1 0.7 copy-start.12
  546.7 11.7 %copy-start.14 = (f32[256,256]{1,0:T(8,128)}, f32[256,256]{1,0:T(8,128)S(1)}, u32[]{:S(2)}) copy-start(f32[256,256]{1,0:T(8,128)S(1)} %fusion.14) | copy-start | bytes 786436
  609.1 2.4 copy-start.2
  613.6 2.2 copy-start.3
  615.8 4.5 copy-start.7
  709.4 0.7 copy-start.15
  774.4 2.4 copy-start.8
Sparse Core Ops, SparseCore 0:
  18.1 80.5 all-reduce.8
  103.0 138.0 all-reduce.10
  313.0 152.1 all-reduce.14
  470.1 74.3 all-reduce.12
  620.4 86.9 all-reduce.16
